TPU v7x, 32 devices: a whole 2x2x4 slice. The times are simulated.
32 devices in a mesh: ctx: 8 (over z, y), fsdp: 4 (over x, core).
Axes of the slice: x: 2, y: 2, z: 4, core: 2. Of those that a mesh axis runs over, the one named last changes fastest.
Arguments:
- tokens: bfloat16 [3, 4, 2048, 1024], P(None, 'fsdp', 'ctx'), may hold values from -6 to 6
- w_router: float32 [1024], replicated, may hold values from -0.1875 to 0.1875
- gain_attn: float32 [1024], replicated, may hold values from 0.1 to 1.9
- w_qkv: bfloat16 [1024, 3072], P('fsdp'), may hold values from -0.1875 to 0.1875
- w_out: bfloat16 [1024, 1024], P('fsdp'), may hold values from -1 to 1
- gain_mlp: float32 [1024], replicated, may hold values from 0.1 to 1.9
- w_up: bfloat16 [1024, 4096], P('fsdp'), may hold values from -0.1875 to 0.1875
- w_down: bfloat16 [4096, 1024], P('fsdp'), may hold values from -0.09375 to 0.09375
- routed: int32 [3, 4, 256], P(None, 'fsdp', 'ctx'), may hold values from 0 to 2047, as said below
- deal: int32 [16], replicated, may hold values from 0 to 15, as said below
- cotangent: bfloat16 [3, 4, 2048, 1024], P(None, 'fsdp', 'ctx'), may hold values from -6 to 6
Outputs:
- output: bfloat16 [3, 4, 2048, 1024], P(None, 'fsdp', 'ctx')
- input_grad: bfloat16 [3, 4, 2048, 1024], P(None, 'fsdp', 'ctx')
- grad_router: float32 [1024], P(('ctx', 'fsdp'))
- grad_gain_attn: float32 [1024], P(('ctx', 'fsdp'))
- grad_qkv: float32 [1024, 3072], P(('ctx', 'fsdp'))
- grad_out: float32 [1024, 1024], P(('ctx', 'fsdp'))
- grad_gain_mlp: float32 [1024], P(('ctx', 'fsdp'))
- grad_up: float32 [1024, 4096], P(('ctx', 'fsdp'))
- grad_down: float32 [4096, 1024], P(('ctx', 'fsdp'))
Inputs may be any that keep to these rules, and one draw needn't show every extreme that they name: `routed`: for each micro-batch and sequence the indices rise; entries j * 32 to (j + 1) * 32 - 1 are distinct stored rows among j * 256 to (j + 1) * 256 - 1, and include j * 256 and (j + 1) * 256 - 1. `deal`: each initial span appears once; stored spans 2 j and 2 j + 1 hold initial spans c and 15 - c.
All inputs are finite; a program needn't handle non-finite values.
Results may differ from a plain program's by a relative error of at most 0.012.
Values may be sent and summed in bfloat16 or wider, within the bound.
No kernel may reach another device: no remote copies, remote signals or barrier semaphores. Data moves between devices by JAX's collectives and lax.ppermute only.
A program may use at most 256 MiB of HBM per device.

v0:
```python
import jax
import jax.numpy as jnp
from jax import lax
from jax.sharding import PartitionSpec as P

HEADS = 16
HEAD_DIM = 64
BLOCK = 256
EPSILON = 1e-06
MASKED = -1e30
HIGHEST = lax.Precision.HIGHEST


def rms_norm(values, gain):
    factor = lax.rsqrt(jnp.mean(values * values, axis=-1, keepdims=True) + EPSILON)
    return values * factor * gain


def exact_gelu(values):
    return jax.nn.gelu(values, approximate=False)


def fetch(w_qkv, w_out, w_up, w_down):
    return (
        lax.all_gather(w_qkv, "fsdp", axis=0, tiled=True),
        lax.all_gather(w_out, "fsdp", axis=0, tiled=True),
        lax.all_gather(w_up, "fsdp", axis=0, tiled=True),
        lax.all_gather(w_down, "fsdp", axis=0, tiled=True),
    )


def lookup(table, index):
    hits = index[..., None] == jnp.arange(table.shape[0], dtype=jnp.int32)
    return jnp.sum(jnp.where(hits, table, 0), axis=-1)


def outer_sum(left, right):
    return lax.dot_general(
        left, right, (((0,), (0,)), ((), ())), preferred_element_type=jnp.float32
    )


def gather_rows(pieces, column):
    return jnp.concatenate([piece[column] for piece in pieces], axis=0)


def shards(
    tokens, w_router, gain_attn, w_qkv, w_out, gain_mlp, w_up, w_down, routed, deal, cotangent
):
    micros, tok_dev, width = (tokens.shape[0], tokens.shape[2], tokens.shape[3])
    span = tok_dev // 2
    rank = lax.axis_index("ctx")
    storage = routed[:, 0, :]
    local_rows = storage - rank * tok_dev
    anchor = lookup(deal, storage // span) * span + storage % span
    own_blocks = anchor // BLOCK
    all_blocks = lax.all_gather(own_blocks, "ctx", axis=1, tiled=True)
    factor = HEAD_DIM ** (-0.5)
    outputs, in_grads, kept = ([], [], [])
    sum_router = jnp.zeros((width,), jnp.float32)
    sum_gain_attn = jnp.zeros((width,), jnp.float32)
    sum_gain_mlp = jnp.zeros((width,), jnp.float32)
    for micro in range(micros):
        full_qkv, full_out, full_up, full_down = fetch(w_qkv, w_out, w_up, w_down)
        resid = tokens[micro, 0].astype(jnp.float32)
        grad_in = cotangent[micro, 0].astype(jnp.float32)
        rows_index = local_rows[micro]
        rows = jnp.take(resid, rows_index, axis=0)
        count = rows.shape[0]
        gate = jax.nn.sigmoid(jnp.dot(rows, w_router, precision=HIGHEST))
        norm1, norm1_back = jax.vjp(rms_norm, rows, gain_attn)
        norm1_low = norm1.astype(jnp.bfloat16)
        qkv = jnp.dot(norm1_low, full_qkv, preferred_element_type=jnp.float32).astype(jnp.bfloat16)
        queries = qkv[:, :width]
        keys_local = qkv[:, width : 2 * width]
        values_local = qkv[:, 2 * width :]
        keys_all, values_all = (
            lax.all_gather(keys_local, "ctx", axis=0, tiled=True),
            lax.all_gather(values_local, "ctx", axis=0, tiled=True),
        )
        total = keys_all.shape[0]
        query_heads = queries.reshape(count, HEADS, HEAD_DIM)
        key_heads = keys_all.reshape(total, HEADS, HEAD_DIM)
        value_heads = values_all.reshape(total, HEADS, HEAD_DIM)
        visible = all_blocks[micro][None, :] <= own_blocks[micro][:, None]
        scores = (
            jnp.einsum("qhd,khd->hqk", query_heads, key_heads, preferred_element_type=jnp.float32)
            * factor
        )
        scores = jnp.where(visible[None], scores, MASKED)
        probs = jax.nn.softmax(scores, axis=-1)
        probs_low = probs.astype(jnp.bfloat16)
        attended = jnp.einsum(
            "hqk,khd->qhd", probs_low, value_heads, preferred_element_type=jnp.float32
        )
        attended_low = attended.reshape(count, width).astype(jnp.bfloat16)
        attn = jnp.dot(attended_low, full_out, preferred_element_type=jnp.float32)
        mid = rows + attn
        norm2, norm2_back = jax.vjp(rms_norm, mid, gain_mlp)
        norm2_low = norm2.astype(jnp.bfloat16)
        hidden = jnp.dot(norm2_low, full_up, preferred_element_type=jnp.float32)
        act, gelu_back = jax.vjp(exact_gelu, hidden)
        act_low = act.astype(jnp.bfloat16)
        mlp = jnp.dot(act_low, full_down, preferred_element_type=jnp.float32)
        branch = attn + mlp
        outputs.append(resid.at[rows_index].set(rows + gate[:, None] * branch).astype(jnp.bfloat16))
        cot_rows = jnp.take(grad_in, rows_index, axis=0)
        d_branch = gate[:, None] * cot_rows
        d_mlp = d_branch.astype(jnp.bfloat16)
        d_logit = jnp.sum(cot_rows * branch, axis=-1) * gate * (1.0 - gate)
        d_act = jnp.dot(d_mlp, full_down.T, preferred_element_type=jnp.float32)
        d_hidden = gelu_back(d_act)[0].astype(jnp.bfloat16)
        d_norm2 = jnp.dot(d_hidden, full_up.T, preferred_element_type=jnp.float32)
        d_mid, d_gain2 = norm2_back(d_norm2)
        d_attn = (d_branch + d_mid).astype(jnp.bfloat16)
        d_attended = jnp.dot(d_attn, full_out.T, preferred_element_type=jnp.float32).astype(
            jnp.bfloat16
        )
        d_heads = d_attended.reshape(count, HEADS, HEAD_DIM)
        d_probs = jnp.einsum(
            "qhd,khd->hqk", d_heads, value_heads, preferred_element_type=jnp.float32
        )
        weighted = jnp.sum(probs * d_probs, axis=-1, keepdims=True)
        d_scores = (probs * (d_probs - weighted)).astype(jnp.bfloat16)
        d_query = (
            jnp.einsum("hqk,khd->qhd", d_scores, key_heads, preferred_element_type=jnp.float32)
            * factor
        )
        d_key_part = (
            jnp.einsum("hqk,qhd->khd", d_scores, query_heads, preferred_element_type=jnp.float32)
            * factor
        )
        d_value_part = jnp.einsum(
            "hqk,qhd->khd", probs_low, d_heads, preferred_element_type=jnp.float32
        )
        d_keys, d_values = (
            lax.psum_scatter(
                d_key_part.reshape(total, width), "ctx", scatter_dimension=0, tiled=True
            ),
            lax.psum_scatter(
                d_value_part.reshape(total, width), "ctx", scatter_dimension=0, tiled=True
            ),
        )
        d_qkv = jnp.concatenate([d_query.reshape(count, width), d_keys, d_values], axis=1).astype(
            jnp.bfloat16
        )
        d_norm1 = jnp.dot(d_qkv, full_qkv.T, preferred_element_type=jnp.float32)
        d_rows_norm, d_gain1 = norm1_back(d_norm1)
        d_rows = cot_rows + d_mid + d_rows_norm + d_logit[:, None] * w_router
        in_grads.append(grad_in.at[rows_index].set(d_rows).astype(jnp.bfloat16))
        sum_router = sum_router + jnp.dot(d_logit, rows, precision=HIGHEST)
        sum_gain_attn = sum_gain_attn + d_gain1
        sum_gain_mlp = sum_gain_mlp + d_gain2
        kept.append((norm1_low, d_qkv, attended_low, d_attn, norm2_low, d_hidden, act_low, d_mlp))
    stacked_rows = tuple((gather_rows(kept, column) for column in range(8)))
    grad_qkv = outer_sum(stacked_rows[0], stacked_rows[1])
    grad_out = outer_sum(stacked_rows[2], stacked_rows[3])
    grad_up = outer_sum(stacked_rows[4], stacked_rows[5])
    grad_down = outer_sum(stacked_rows[6], stacked_rows[7])
    summed = (
        lax.psum_scatter(sum_router, ("ctx", "fsdp"), scatter_dimension=0, tiled=True),
        lax.psum_scatter(sum_gain_attn, ("ctx", "fsdp"), scatter_dimension=0, tiled=True),
        lax.psum_scatter(grad_qkv, ("ctx", "fsdp"), scatter_dimension=0, tiled=True),
        lax.psum_scatter(grad_out, ("ctx", "fsdp"), scatter_dimension=0, tiled=True),
        lax.psum_scatter(sum_gain_mlp, ("ctx", "fsdp"), scatter_dimension=0, tiled=True),
        lax.psum_scatter(grad_up, ("ctx", "fsdp"), scatter_dimension=0, tiled=True),
        lax.psum_scatter(grad_down, ("ctx", "fsdp"), scatter_dimension=0, tiled=True),
    )
    output = jnp.stack(outputs)[:, None]
    input_grad = jnp.stack(in_grads)[:, None]
    return (
        output,
        input_grad,
        summed[0],
        summed[1],
        summed[2],
        summed[3],
        summed[4],
        summed[5],
        summed[6],
    )


def solution(mesh):
    placed = (
        P(None, "fsdp", "ctx", None),
        P(),
        P(),
        P("fsdp", None),
        P("fsdp", None),
        P(),
        P("fsdp", None),
        P("fsdp", None),
        P(None, "fsdp", "ctx"),
        P(),
        P(None, "fsdp", "ctx", None),
    )
    return jax.shard_map(
        shards,
        mesh=mesh,
        in_specs=placed,
        out_specs=(
            P(None, "fsdp", "ctx", None),
            P(None, "fsdp", "ctx", None),
            P(("ctx", "fsdp")),
            P(("ctx", "fsdp")),
            P(("ctx", "fsdp"), None),
            P(("ctx", "fsdp"), None),
            P(("ctx", "fsdp")),
            P(("ctx", "fsdp"), None),
            P(("ctx", "fsdp"), None),
        ),
        check_vma=False,
    )
```

profile of v0, /device:TPU:14, one launch (start us, length us, event | category | flops | bytes accessed | tf_op | source)
XLA Modules:
  0.0 1517.1 jit_solution(7598239076845456931)
XLA Ops:
  10.8 25.0 %all-gather = s32[8,32,3]{1,2,0:T(4,128)S(1)} all-gather(s32[1,32,3]{1,2,0:T(4,128)S(1)} %bitcast.289), channel_id=1, replica_groups=mesh['ctx'=8,'fsdp'=4] {'ctx'}, dimensions={0}, use_global_device_ids=true | all-gather | bytes 3456 | tf_op jit(solution)/shard_map/all_gather | solution.py:57
  46.3 9.9 all-gather.6.cloned.1.call-done
  60.4 29.6 %all_gather.44 = bf16[256,1024]{1,0:T(8,128)(2,1)S(1)} all-gather(bf16[32,1024]{1,0:T(8,128)(2,1)S(1)} %get-tuple-element.89), channel_id=1, replica_groups=mesh['ctx'=8,'fsdp'=4] {'ctx'}, dimensions={0}, use_global_device_ids=true | all-gather | bytes 589824 | tf_op jit(solution)/shard_map/all_gather | solution.py:78
  90.2 31.1 %all_gather.42 = bf16[256,1024]{1,0:T(8,128)(2,1)S(1)} all-gather(bf16[32,1024]{1,0:T(8,128)(2,1)S(1)} %get-tuple-element.90), channel_id=1, replica_groups=mesh['ctx'=8,'fsdp'=4] {'ctx'}, dimensions={0}, use_global_device_ids=true | all-gather | bytes 589824 | tf_op jit(solution)/shard_map/all_gather | solution.py:79
  127.5 12.7 all-gather.10.cloned.1.call-done
  140.3 4.9 fusion.285
  145.2 54.8 %all-gather.12.cloned.1.call-done = bf16[4096,1024]{1,0:T(8,128)(2,1)} async-done(((bf16[1024,1024]{1,0:T(8,128)(2,1)}), bf16[4096,1024]{1,0:T(8,128)(2,1)}) %all-gather.12.cloned.1.call-update) | async-done | bytes 8388624 | tf_op jit(solution)/shard_map/all_gather | solution.py:28
  200.0 7.5 add_convert_fusion.2
  249.8 5.6 convolution_add_fusion.2
  255.4 27.9 %reduce-scatter.13.cloned.1.call-done = f32[32,1024]{1,0:T(8,128)} async-done(((f32[256,1024]{1,0:T(8,128)}), f32[32,1024]{1,0:T(8,128)}) %reduce-scatter.13.cloned.1.call-update) | async-done | bytes 131088 | tf_op jit(solution)/shard_map/reduce_scatter | solution.py:140
  284.9 64.6 %reduce-scatter.11.cloned.1.call-done = f32[32,1024]{1,0:T(8,128)} async-done(((f32[256,1024]{1,0:T(8,128)}), f32[32,1024]{1,0:T(8,128)}) %reduce-scatter.11.cloned.1.call-update) | async-done | bytes 131088 | tf_op jit(solution)/shard_map/reduce_scatter | solution.py:137
  350.4 6.3 multiply_reduce_fusion.8
  369.3 29.4 %all_gather.51 = bf16[256,1024]{1,0:T(8,128)(2,1)} all-gather(bf16[32,1024]{1,0:T(8,128)(2,1)} %get-tuple-element.95), channel_id=1, replica_groups=mesh['ctx'=8,'fsdp'=4] {'ctx'}, dimensions={0}, use_global_device_ids=true | all-gather | bytes 589824 | tf_op jit(solution)/shard_map/all_gather | solution.py:78
  400.7 34.1 %all_gather.50 = bf16[256,1024]{1,0:T(8,128)(2,1)} all-gather(bf16[32,1024]{1,0:T(8,128)(2,1)} %get-tuple-element.96), channel_id=1, replica_groups=mesh['ctx'=8,'fsdp'=4] {'ctx'}, dimensions={0}, use_global_device_ids=true | all-gather | bytes 589824 | tf_op jit(solution)/shard_map/all_gather | solution.py:79
  436.8 33.5 %all_gather.49 = bf16[256,1024]{1,0:T(8,128)(2,1)} all-gather(bf16[32,1024]{1,0:T(8,128)(2,1)} %get-tuple-element.92), channel_id=1, replica_groups=mesh['ctx'=8,'fsdp'=4] {'ctx'}, dimensions={0}, use_global_device_ids=true | all-gather | bytes 589824 | tf_op jit(solution)/shard_map/all_gather | solution.py:78
  472.4 33.4 %all_gather.48 = bf16[256,1024]{1,0:T(8,128)(2,1)} all-gather(bf16[32,1024]{1,0:T(8,128)(2,1)} %get-tuple-element.93), channel_id=1, replica_groups=mesh['ctx'=8,'fsdp'=4] {'ctx'}, dimensions={0}, use_global_device_ids=true | all-gather | bytes 589824 | tf_op jit(solution)/shard_map/all_gather | solution.py:79
  533.5 5.1 fusion.286
  538.6 7.6 add_convert_fusion.1
  591.8 44.8 %reduce-scatter.17.cloned.1.call-done = f32[32,1024]{1,0:T(8,128)} async-done(((f32[256,1024]{1,0:T(8,128)}), f32[32,1024]{1,0:T(8,128)}) %reduce-scatter.17.cloned.1.call-update) | async-done | bytes 131088 | tf_op jit(solution)/shard_map/reduce_scatter | solution.py:140
  637.5 65.4 %reduce-scatter.21.cloned.1.call-done = f32[32,1024]{1,0:T(8,128)} async-done(((f32[256,1024]{1,0:T(8,128)}), f32[32,1024]{1,0:T(8,128)}) %reduce-scatter.21.cloned.1.call-update) | async-done | bytes 131088 | tf_op jit(solution)/shard_map/reduce_scatter | solution.py:140
  703.8 65.0 %reduce-scatter.15.cloned.1.call-done = f32[32,1024]{1,0:T(8,128)} async-done(((f32[256,1024]{1,0:T(8,128)}), f32[32,1024]{1,0:T(8,128)}) %reduce-scatter.15.cloned.1.call-update) | async-done | bytes 131088 | tf_op jit(solution)/shard_map/reduce_scatter | solution.py:137
  769.8 65.2 %reduce-scatter.19.cloned.1.call-done = f32[32,1024]{1,0:T(8,128)} async-done(((f32[256,1024]{1,0:T(8,128)}), f32[32,1024]{1,0:T(8,128)}) %reduce-scatter.19.cloned.1.call-update) | async-done | bytes 131088 | tf_op jit(solution)/shard_map/reduce_scatter | solution.py:137
  835.9 6.4 fusion.45
  845.7 8.2 fusion.39
  855.0 8.1 fusion.33
  866.5 5.1 convolution_add_fusion.1
  873.8 5.8 convolution_add_fusion
  891.7 4.9 fusion.93
  905.1 39.6 %all-reduce.3 = (f32[1024]{0:T(1024)S(1)}, f32[1024]{0:T(1024)S(1)}, f32[1024]{0:T(1024)S(1)}) all-reduce(f32[1024]{0:T(1024)S(1)} %add_add_fusion.11, f32[1024]{0:T(1024)S(1)} %add_add_fusion.10, f32[1024]{0:T(1024)} %add_add_fusion.9), channel_id=8, replica_groups=mesh['ctx'=8,'fsdp'=4] {'ctx','fsdp'}, use_global_device_ids=true, to_apply=%region_37.39.clone | all-reduce | flops 3072 | bytes 24576
  950.4 185.2 %reduce-scatter.23.cloned.1.call-done = f32[32,3072]{1,0:T(8,128)} async-done(((f32[1024,3072]{1,0:T(8,128)}), f32[32,3072]{1,0:T(8,128)}) %reduce-scatter.23.cloned.1.call-update) | async-done | bytes 393232 | tf_op jit(solution)/shard_map/reduce_scatter | solution.py:163
  1135.5 187.4 %reduce-scatter.29.cloned.1.call-done = f32[128,1024]{1,0:T(8,128)} async-done(((f32[4096,1024]{1,0:T(8,128)}), f32[128,1024]{1,0:T(8,128)}) %reduce-scatter.29.cloned.1.call-update) | async-done | bytes 524304 | tf_op jit(solution)/shard_map/reduce_scatter | solution.py:167
  1323.0 187.3 %reduce-scatter.27.cloned.1.call-done = f32[32,4096]{1,0:T(8,128)} async-done(((f32[1024,4096]{1,0:T(8,128)}), f32[32,4096]{1,0:T(8,128)}) %reduce-scatter.27.cloned.1.call-update) | async-done | bytes 524304 | tf_op jit(solution)/shard_map/reduce_scatter | solution.py:166
  (490 shorter events, 199.7 us)
Async XLA Ops:
  7.2 49.0 %all-gather.6.cloned.1.call-start = ((), (), s32[]{:S(2)}) async-start(), calls=%async_computation.10 | async-start | bytes 7864320 | tf_op jit(solution)/shard_map/all_gather | solution.py:25
  7.9 116.5 %all-gather.8.cloned.1.call-start = ((), (), s32[]{:S(2)}) async-start(), calls=%async_computation.11 | async-start | bytes 2621440 | tf_op jit(solution)/shard_map/all_gather | solution.py:26
  8.7 131.6 %all-gather.10.cloned.1.call-start = ((), (), s32[]{:S(2)}) async-start(), calls=%async_computation.12 | async-start | bytes 10485760 | tf_op jit(solution)/shard_map/all_gather | solution.py:27
  9.4 190.6 %all-gather.12.cloned.1.call-start = ((), (), s32[]{:S(2)}) async-start(), calls=%async_computation.13 | async-start | bytes 10485760 | tf_op jit(solution)/shard_map/all_gather | solution.py:28
  10.0 273.3 %reduce-scatter.13.cloned.1.call-start = ((), (), s32[]{:S(2)}) async-start(), calls=%async_computation.15 | async-start | bytes 1179648 | tf_op jit(solution)/shard_map/reduce_scatter | solution.py:140
  43.8 167.0 %copy-start.22 = (f32[32,1024]{1,0:T(8,128)}, f32[32,1024]{1,0:T(8,128)S(1)}, u32[]{:S(2)}) copy-start(f32[32,1024]{1,0:T(8,128)S(1)} %gather_fusion.3) | copy-start | bytes 393220
  46.2 78.3 %copy-start.123 = (f32[32]{0:T(128)}, f32[32]{0:T(128)S(1)}, u32[]{:S(2)}) copy-start(f32[32]{0:T(128)S(1)} %fusion.32) | copy-start | bytes 388
  60.4 63.9 %copy-start.47 = (bf16[32,16,64]{2,1,0:T(8,128)(2,1)}, bf16[32,16,64]{2,1,0:T(8,128)(2,1)S(1)}, u32[]{:S(2)}) copy-start(bf16[32,16,64]{2,1,0:T(8,128)(2,1)S(1)} %reshape.442) | copy-start | bytes 196612
  127.4 72.6 %copy-start.93 = (bf16[32,1024]{1,0:T(8,128)(2,1)}, bf16[32,1024]{1,0:T(8,128)(2,1)S(1)}, u32[]{:S(2)}) copy-start(bf16[32,1024]{1,0:T(8,128)(2,1)S(1)} %get-tuple-element.122) | copy-start | bytes 196612
  127.4 83.4 %copy-start.23 = (f32[32,1024]{1,0:T(8,128)}, f32[32,1024]{1,0:T(8,128)S(1)}, u32[]{:S(2)}) copy-start(f32[32,1024]{1,0:T(8,128)S(1)} %get-tuple-element.71) | copy-start | bytes 393220
  145.2 62.3 %copy-start.31 = (f32[32,4096]{1,0:T(8,128)}, f32[32,4096]{1,0:T(8,128)S(1)}, u32[]{:S(2)}) copy-start(f32[32,4096]{1,0:T(8,128)S(1)} %fusion.285) | copy-start | bytes 1572868
  218.9 130.5 %reduce-scatter.11.cloned.1.call-start = ((), (), s32[]{:S(2)}) async-start(), calls=%async_computation.14 | async-start | bytes 1179648 | tf_op jit(solution)/shard_map/reduce_scatter | solution.py:137
  241.6 395.0 %reduce-scatter.17.cloned.1.call-start = ((), (), s32[]{:S(2)}) async-start(), calls=%async_computation.17 | async-start | bytes 1179648 | tf_op jit(solution)/shard_map/reduce_scatter | solution.py:140
  569.6 133.3 %reduce-scatter.21.cloned.1.call-start = ((), (), s32[]{:S(2)}) async-start(), calls=%async_computation.19 | async-start | bytes 1179648 | tf_op jit(solution)/shard_map/reduce_scatter | solution.py:140
  578.9 190.0 %reduce-scatter.15.cloned.1.call-start = ((), (), s32[]{:S(2)}) async-start(), calls=%async_computation.16 | async-start | bytes 1179648 | tf_op jit(solution)/shard_map/reduce_scatter | solution.py:137
  581.9 253.1 %reduce-scatter.19.cloned.1.call-start = ((), (), s32[]{:S(2)}) async-start(), calls=%async_computation.18 | async-start | bytes 1179648 | tf_op jit(solution)/shard_map/reduce_scatter | solution.py:137
  586.8 363.5 %reduce-scatter.25.cloned.1.call-start = ((), (), s32[]{:S(2)}) async-start(), calls=%async_computation.21 | async-start | bytes 4325376 | tf_op jit(solution)/shard_map/reduce_scatter | solution.py:164
  590.7 245.2 %copy-start.62 = (bf16[32,1024]{1,0:T(8,128)(2,1)S(1)}, bf16[32,1024]{1,0:T(8,128)(2,1)}, u32[]{:S(2)}) copy-start(bf16[32,1024]{1,0:T(8,128)(2,1)} %copy-done.61) | copy-start | bytes 196612
  590.7 245.2 %copy-start.63 = (bf16[32,1024]{1,0:T(8,128)(2,1)S(1)}, bf16[32,1024]{1,0:T(8,128)(2,1)}, u32[]{:S(2)}) copy-start(bf16[32,1024]{1,0:T(8,128)(2,1)} %get-tuple-element.98) | copy-start | bytes 196612
  590.7 245.2 %copy-start.65 = (bf16[32,1024]{1,0:T(8,128)(2,1)S(1)}, bf16[32,1024]{1,0:T(8,128)(2,1)}, u32[]{:S(2)}) copy-start(bf16[32,1024]{1,0:T(8,128)(2,1)} %copy-done.64) | copy-start | bytes 196612
  590.7 245.2 %copy-start.66 = (bf16[32,1024]{1,0:T(8,128)(2,1)S(1)}, bf16[32,1024]{1,0:T(8,128)(2,1)}, u32[]{:S(2)}) copy-start(bf16[32,1024]{1,0:T(8,128)(2,1)} %reshape.451) | copy-start | bytes 196612
  590.7 245.2 %copy-start.67 = (bf16[32,1024]{1,0:T(8,128)(2,1)S(1)}, bf16[32,1024]{1,0:T(8,128)(2,1)}, u32[]{:S(2)}) copy-start(bf16[32,1024]{1,0:T(8,128)(2,1)} %convert.41) | copy-start | bytes 196612
  590.7 245.2 %copy-start.69 = (bf16[32,1024]{1,0:T(8,128)(2,1)S(1)}, bf16[32,1024]{1,0:T(8,128)(2,1)}, u32[]{:S(2)}) copy-start(bf16[32,1024]{1,0:T(8,128)(2,1)} %copy-done.68) | copy-start | bytes 196612
  590.8 544.8 %reduce-scatter.23.cloned.1.call-start = ((), (), s32[]{:S(2)}) async-start(), calls=%async_computation.20 | async-start | bytes 12976128 | tf_op jit(solution)/shard_map/reduce_scatter | solution.py:163
  591.3 251.0 %copy-start.72 = (bf16[32,1024]{1,0:T(8,128)(2,1)}, bf16[32,1024]{1,0:T(8,128)(2,1)S(1)}, u32[]{:S(2)}) copy-start(bf16[32,1024]{1,0:T(8,128)(2,1)S(1)} %reshape.459) | copy-start | bytes 196612
  591.8 250.5 %copy-start.70 = (bf16[32,1024]{1,0:T(8,128)(2,1)}, bf16[32,1024]{1,0:T(8,128)(2,1)S(1)}, u32[]{:S(2)}) copy-start(bf16[32,1024]{1,0:T(8,128)(2,1)S(1)} %reshape.455) | copy-start | bytes 196612
  637.5 204.8 %copy-start.74 = (bf16[32,1024]{1,0:T(8,128)(2,1)}, bf16[32,1024]{1,0:T(8,128)(2,1)S(1)}, u32[]{:S(2)}) copy-start(bf16[32,1024]{1,0:T(8,128)(2,1)S(1)} %convert.44) | copy-start | bytes 196612
  703.8 138.5 %copy-start.78 = (bf16[32,1024]{1,0:T(8,128)(2,1)}, bf16[32,1024]{1,0:T(8,128)(2,1)S(1)}, u32[]{:S(2)}) copy-start(bf16[32,1024]{1,0:T(8,128)(2,1)S(1)} %convert.47) | copy-start | bytes 196612
  769.8 72.5 %copy-start.76 = (bf16[32,1024]{1,0:T(8,128)(2,1)}, bf16[32,1024]{1,0:T(8,128)(2,1)S(1)}, u32[]{:S(2)}) copy-start(bf16[32,1024]{1,0:T(8,128)(2,1)S(1)} %convert.43) | copy-start | bytes 196612
  842.4 480.5 %reduce-scatter.29.cloned.1.call-start = ((), (), s32[]{:S(2)}) async-start(), calls=%async_computation.23 | async-start | bytes 17301504 | tf_op jit(solution)/shard_map/reduce_scatter | solution.py:167
  853.9 656.4 %reduce-scatter.27.cloned.1.call-start = ((), (), s32[]{:S(2)}) async-start(), calls=%async_computation.22 | async-start | bytes 17301504 | tf_op jit(solution)/shard_map/reduce_scatter | solution.py:166
  896.8 50.4 %copy-start.25 = (f32[32,1024]{1,0:T(8,128)S(1)}, f32[32,1024]{1,0:T(8,128)}, u32[]{:S(2)}) copy-start(f32[32,1024]{1,0:T(8,128)} %get-tuple-element.75) | copy-start | bytes 393220
  (134 other events, 848.7 us)
Sparse Core Ops, SparseCore 0:
  9.6 46.5 all-gather.5
  57.8 22.5 all-gather.7
  81.9 58.2 all-gather.9
  141.7 58.2 all-gather.11
  219.0 64.2 reduce-scatter.12
  287.0 62.4 reduce-scatter.10
  569.7 66.7 reduce-scatter.16
  640.4 62.4 reduce-scatter.20
  706.3 62.5 reduce-scatter.14
  772.5 62.4 reduce-scatter.18
  837.8 107.5 reduce-scatter.24
  951.9 183.5 reduce-scatter.22
  1138.5 184.4 reduce-scatter.28
  1325.8 184.4 reduce-scatter.26
where the time goes:
time: 1520 us
  waiting for transfers between devices  973 us (64%)
  blocking collectives  256 us (17%)
  matrix products  154 us (10%)
  local copies, waits for them, and re-layouts  63.5 us (4%)
  other arithmetic  53.5 us (4%)
  between operations  16.2 us (1%)
    reduce_scatter x3, waiting for transfers between devices, shards(): lax.psum_scatter(d_key_part.reshape(total, width), 'ctx', scatter_dimensi...  195 us
    reduce_scatter x1, waiting for transfers between devices, shards(): lax.psum_scatter(grad_down, ('ctx', 'fsdp'), scatter_dimension=0, tiled=T...  187 us
    reduce_scatter x1, waiting for transfers between devices, shards(): lax.psum_scatter(grad_up, ('ctx', 'fsdp'), scatter_dimension=0, tiled=True)  187 us
    reduce_scatter x1, waiting for transfers between devices, shards(): lax.psum_scatter(grad_qkv, ('ctx', 'fsdp'), scatter_dimension=0, tiled=True)  185 us
    reduce_scatter x3, waiting for transfers between devices, shards(): lax.psum_scatter(d_value_part.reshape(total, width), 'ctx', scatter_dimen...  138 us
    all_gather x3, blocking collectives, shards(): lax.all_gather(values_local, 'ctx', axis=0, tiled=True)  98.5 us
    all_gather x3, blocking collectives, shards(): lax.all_gather(keys_local, 'ctx', axis=0, tiled=True)  92.5 us
    all_gather x1, waiting for transfers between devices, fetch(): lax.all_gather(w_down, 'fsdp', axis=0, tiled=True)  54.8 us
  transfers between devices with their start and end apart: 14, of which 12 were waited for; matrix products, arithmetic and copies ran while one was open for 10% of the time, Pallas kernels for 0%

commit v1 on v0

--- a/solution.py
+++ b/solution.py
@@ -9,6 +9,28 @@
 EPSILON = 1e-06
 MASKED = -1e30
 HIGHEST = lax.Precision.HIGHEST
+
+
+def laid_out(pieces, dim):
+    lengths = list(pieces.shape[1:])
+    lengths[dim] *= pieces.shape[0]
+    return jnp.moveaxis(pieces, 0, dim).reshape(lengths)
+
+
+def collect(array, axis, dim):
+    size = lax.axis_size(axis)
+    pairs = [(i, (i + 1) % size) for i in range(size)]
+    back = [(b, a) for a, b in pairs]
+    lower, upper = ([], [])
+    for step in range(size - 1):
+        if step % 2 == 0:
+            lower.append(lax.ppermute(lower[-1] if lower else array, axis, pairs))
+        else:
+            upper.append(lax.ppermute(upper[-1] if upper else array, axis, back))
+    tiles = jnp.stack([*lower[::-1], array, *upper])
+    shift = lax.axis_index(axis) - len(lower)
+    tiles = tiles[(jnp.arange(size) - shift) % size]
+    return laid_out(tiles, dim)
 
 
 def rms_norm(values, gain):
@@ -75,7 +97,7 @@
         keys_local = qkv[:, width : 2 * width]
         values_local = qkv[:, 2 * width :]
         keys_all, values_all = (
-            lax.all_gather(keys_local, "ctx", axis=0, tiled=True),
+            collect(keys_local, "ctx", 0),
             lax.all_gather(values_local, "ctx", axis=0, tiled=True),
         )
         total = keys_all.shape[0]

time: 1520 us -> 1510 us (level)
  blocking collectives: 256 us -> 167 us
  local copies, waits for them, and re-layouts: 63.5 us -> 102 us
  starting transfers between devices: 1.18 us -> 29.7 us
    all_gather x3 -> x0, blocking collectives: 92.5 us -> none  [shards(): lax.all_gather(keys_local, 'ctx', axis=0, tiled=True)]
    ppermute x0 -> x21, starting transfers between devices: none -> 28.8 us  [the longest x12 17.2 us: collect(): lower.append(lax.ppermute(lower[-1] if lower else array, axis, pairs))]
    unnamed x308 -> x321, local copies, waits for them, and re-layouts: 14.5 us -> 35.9 us
  transfers between devices with their start and end apart: 14 -> 35, of which waited for: 12 -> 17; matrix products, arithmetic and copies ran while one was open for 10% -> 14% of each run, Pallas kernels for 0% -> 0%
where the time goes in v1:
time: 1510 us
  waiting for transfers between devices  976 us (65%)
  blocking collectives  167 us (11%)
  matrix products  156 us (10%)
  local copies, waits for them, and re-layouts  102 us (7%)
  other arithmetic  61.7 us (4%)
  starting transfers between devices  29.7 us (2%)
  between operations  16.1 us (1%)
    reduce_scatter x3, waiting for transfers between devices, shards(): lax.psum_scatter(d_key_part.reshape(total, width), 'ctx', scatter_dimensi...  195 us
    reduce_scatter x1, waiting for transfers between devices, shards(): lax.psum_scatter(grad_down, ('ctx', 'fsdp'), scatter_dimension=0, tiled=T...  187 us
    reduce_scatter x1, waiting for transfers between devices, shards(): lax.psum_scatter(grad_up, ('ctx', 'fsdp'), scatter_dimension=0, tiled=True)  187 us
    reduce_scatter x1, waiting for transfers between devices, shards(): lax.psum_scatter(grad_qkv, ('ctx', 'fsdp'), scatter_dimension=0, tiled=True)  178 us
    reduce_scatter x3, waiting for transfers between devices, shards(): lax.psum_scatter(d_value_part.reshape(total, width), 'ctx', scatter_dimen...  140 us
    all_gather x3, blocking collectives, shards(): lax.all_gather(values_local, 'ctx', axis=0, tiled=True)  102 us
    all_gather x1, waiting for transfers between devices, fetch(): lax.all_gather(w_down, 'fsdp', axis=0, tiled=True)  54.8 us
    unnamed x1, blocking collectives  39.9 us
  transfers between devices with their start and end apart: 35, of which 17 were waited for; matrix products, arithmetic and copies ran while one was open for 14% of the time, Pallas kernels for 0%

profile of v1, /device:TPU:14, one launch (start us, length us, event | category | flops | bytes accessed | tf_op | source)
XLA Modules:
  0.0 1508.0 jit_solution(3940499111331921191)
XLA Ops:
  10.2 25.0 %all-gather = s32[8,32,3]{1,2,0:T(4,128)S(1)} all-gather(s32[1,32,3]{1,2,0:T(4,128)S(1)} %bitcast.330), channel_id=1, replica_groups=mesh['ctx'=8,'fsdp'=4] {'ctx'}, dimensions={0}, use_global_device_ids=true | all-gather | bytes 3456 | tf_op jit(solution)/shard_map/all_gather | solution.py:79
  43.3 12.9 all-gather.6.cloned.1.call-done
  78.2 33.4 %all_gather.33 = bf16[256,1024]{1,0:T(8,128)(2,1)S(1)} all-gather(bf16[32,1024]{1,0:T(8,128)(2,1)} %get-tuple-element.90), channel_id=1, replica_groups=mesh['ctx'=8,'fsdp'=4] {'ctx'}, dimensions={0}, use_global_device_ids=true | all-gather | bytes 589824 | tf_op jit(solution)/shard_map/all_gather | solution.py:101
  127.6 12.7 all-gather.10.cloned.1.call-done
  140.3 4.9 fusion.287
  145.3 54.8 %all-gather.12.cloned.1.call-done = bf16[4096,1024]{1,0:T(8,128)(2,1)} async-done(((bf16[1024,1024]{1,0:T(8,128)(2,1)}), bf16[4096,1024]{1,0:T(8,128)(2,1)}) %all-gather.12.cloned.1.call-update) | async-done | bytes 8388624 | tf_op jit(solution)/shard_map/all_gather | solution.py:50
  200.0 7.5 add_convert_fusion.2
  248.4 5.6 convolution_add_fusion.2
  254.0 29.4 %reduce-scatter.13.cloned.1.call-done = f32[32,1024]{1,0:T(8,128)} async-done(((f32[256,1024]{1,0:T(8,128)}), f32[32,1024]{1,0:T(8,128)}) %reduce-scatter.13.cloned.1.call-update) | async-done | bytes 131088 | tf_op jit(solution)/shard_map/reduce_scatter | solution.py:162
  284.9 64.6 %reduce-scatter.11.cloned.1.call-done = f32[32,1024]{1,0:T(8,128)} async-done(((f32[256,1024]{1,0:T(8,128)}), f32[32,1024]{1,0:T(8,128)}) %reduce-scatter.11.cloned.1.call-update) | async-done | bytes 131088 | tf_op jit(solution)/shard_map/reduce_scatter | solution.py:159
  350.4 6.3 multiply_reduce_fusion.8
  375.8 33.0 %all_gather.38 = bf16[256,1024]{1,0:T(8,128)(2,1)} all-gather(bf16[32,1024]{1,0:T(8,128)(2,1)S(1)} %get-tuple-element.93), channel_id=1, replica_groups=mesh['ctx'=8,'fsdp'=4] {'ctx'}, dimensions={0}, use_global_device_ids=true | all-gather | bytes 589824 | tf_op jit(solution)/shard_map/all_gather | solution.py:101
  409.0 4.3 collective-permute-start.12
  413.9 35.3 %all_gather.39 = bf16[256,1024]{1,0:T(8,128)(2,1)} all-gather(bf16[32,1024]{1,0:T(8,128)(2,1)S(1)} %get-tuple-element.96), channel_id=1, replica_groups=mesh['ctx'=8,'fsdp'=4] {'ctx'}, dimensions={0}, use_global_device_ids=true | all-gather | bytes 589824 | tf_op jit(solution)/shard_map/all_gather | solution.py:101
  456.7 4.3 collective-permute-start.13
  524.2 5.1 fusion.288
  529.4 7.6 add_convert_fusion.1
  542.5 4.5 add_convert_fusion
  582.7 44.9 %reduce-scatter.17.cloned.1.call-done = f32[32,1024]{1,0:T(8,128)} async-done(((f32[256,1024]{1,0:T(8,128)}), f32[32,1024]{1,0:T(8,128)}) %reduce-scatter.17.cloned.1.call-update) | async-done | bytes 131088 | tf_op jit(solution)/shard_map/reduce_scatter | solution.py:162
  628.6 65.3 %reduce-scatter.21.cloned.1.call-done = f32[32,1024]{1,0:T(8,128)} async-done(((f32[256,1024]{1,0:T(8,128)}), f32[32,1024]{1,0:T(8,128)}) %reduce-scatter.21.cloned.1.call-update) | async-done | bytes 131088 | tf_op jit(solution)/shard_map/reduce_scatter | solution.py:162
  694.8 65.0 %reduce-scatter.15.cloned.1.call-done = f32[32,1024]{1,0:T(8,128)} async-done(((f32[256,1024]{1,0:T(8,128)}), f32[32,1024]{1,0:T(8,128)}) %reduce-scatter.15.cloned.1.call-update) | async-done | bytes 131088 | tf_op jit(solution)/shard_map/reduce_scatter | solution.py:159
  760.6 65.2 %reduce-scatter.19.cloned.1.call-done = f32[32,1024]{1,0:T(8,128)} async-done(((f32[256,1024]{1,0:T(8,128)}), f32[32,1024]{1,0:T(8,128)}) %reduce-scatter.19.cloned.1.call-update) | async-done | bytes 131088 | tf_op jit(solution)/shard_map/reduce_scatter | solution.py:159
  826.9 6.4 fusion.45
  836.8 8.2 fusion.39
  846.1 8.1 fusion.33
  863.6 5.1 convolution_add_fusion.1
  870.1 6.0 convolution_add_fusion
  886.0 4.9 fusion.93
  901.3 39.9 %all-reduce.3 = (f32[1024]{0:T(1024)S(1)}, f32[1024]{0:T(1024)S(1)}, f32[1024]{0:T(1024)S(1)}) all-reduce(f32[1024]{0:T(1024)S(1)} %add_add_fusion.11, f32[1024]{0:T(1024)S(1)} %add_add_fusion.10, f32[1024]{0:T(1024)} %add_add_fusion.9), channel_id=8, replica_groups=mesh['ctx'=8,'fsdp'=4] {'ctx','fsdp'}, use_global_device_ids=true, to_apply=%region_37.39.clone | all-reduce | flops 3072 | bytes 24576
  948.1 178.4 %reduce-scatter.23.cloned.1.call-done = f32[32,3072]{1,0:T(8,128)} async-done(((f32[1024,3072]{1,0:T(8,128)}), f32[32,3072]{1,0:T(8,128)}) %reduce-scatter.23.cloned.1.call-update) | async-done | bytes 393232 | tf_op jit(solution)/shard_map/reduce_scatter | solution.py:185
  1126.5 187.4 %reduce-scatter.29.cloned.1.call-done = f32[128,1024]{1,0:T(8,128)} async-done(((f32[4096,1024]{1,0:T(8,128)}), f32[128,1024]{1,0:T(8,128)}) %reduce-scatter.29.cloned.1.call-update) | async-done | bytes 524304 | tf_op jit(solution)/shard_map/reduce_scatter | solution.py:189
  1313.9 187.3 %reduce-scatter.27.cloned.1.call-done = f32[32,4096]{1,0:T(8,128)} async-done(((f32[1024,4096]{1,0:T(8,128)}), f32[32,4096]{1,0:T(8,128)}) %reduce-scatter.27.cloned.1.call-update) | async-done | bytes 524304 | tf_op jit(solution)/shard_map/reduce_scatter | solution.py:188
  (553 shorter events, 268.6 us)
Async XLA Ops:
  7.2 49.0 %all-gather.6.cloned.1.call-start = ((), (), s32[]{:S(2)}) async-start(), calls=%async_computation.10 | async-start | bytes 7864320 | tf_op jit(solution)/shard_map/all_gather | solution.py:47
  7.9 116.7 %all-gather.8.cloned.1.call-start = ((), (), s32[]{:S(2)}) async-start(), calls=%async_computation.11 | async-start | bytes 2621440 | tf_op jit(solution)/shard_map/all_gather | solution.py:48
  8.7 131.6 %all-gather.10.cloned.1.call-start = ((), (), s32[]{:S(2)}) async-start(), calls=%async_computation.12 | async-start | bytes 10485760 | tf_op jit(solution)/shard_map/all_gather | solution.py:49
  9.4 190.6 %all-gather.12.cloned.1.call-start = ((), (), s32[]{:S(2)}) async-start(), calls=%async_computation.13 | async-start | bytes 10485760 | tf_op jit(solution)/shard_map/all_gather | solution.py:50
  10.0 273.3 %reduce-scatter.13.cloned.1.call-start = ((), (), s32[]{:S(2)}) async-start(), calls=%async_computation.15 | async-start | bytes 1179648 | tf_op jit(solution)/shard_map/reduce_scatter | solution.py:162
  67.8 5.4 collective-permute-start.4
  73.2 39.6 %collective-permute-start.5 = (bf16[32,1024]{1,0:T(8,128)(2,1)S(1)}, bf16[32,1024]{1,0:T(8,128)(2,1)}, u32[]{:S(2)}, u32[]{:S(2)}) collective-permute-start(bf16[32,1024]{1,0:T(8,128)(2,1)S(1)} %collective-permute-done.4), channel_id=1, source_target_pairs={{4,0},{8,4},{12,8},{16,12},{20,16},{24,20},{28,24},{0,28},{5,1},{9... | collective-permute-start | bytes 196616 | tf_op jit(solution)/shard_map/ppermute | solution.py:29
  74.9 38.5 %collective-permute-start.3 = (bf16[32,1024]{1,0:T(8,128)(2,1)S(1)}, bf16[32,1024]{1,0:T(8,128)(2,1)}, u32[]{:S(2)}, u32[]{:S(2)}) collective-permute-start(bf16[32,1024]{1,0:T(8,128)(2,1)S(1)} %collective-permute-done.2), channel_id=1, source_target_pairs={{0,4},{4,8},{8,12},{12,16},{16,20},{20,24},{24,28},{28,0},{1,5},{5... | collective-permute-start | bytes 196616 | tf_op jit(solution)/shard_map/ppermute | solution.py:27
  112.8 6.5 collective-permute-start.6
  218.9 130.6 %reduce-scatter.11.cloned.1.call-start = ((), (), s32[]{:S(2)}) async-start(), calls=%async_computation.14 | async-start | bytes 1179648 | tf_op jit(solution)/shard_map/reduce_scatter | solution.py:159
  240.4 387.2 %reduce-scatter.17.cloned.1.call-start = ((), (), s32[]{:S(2)}) async-start(), calls=%async_computation.17 | async-start | bytes 1179648 | tf_op jit(solution)/shard_map/reduce_scatter | solution.py:162
  361.4 7.4 collective-permute-start.7
  367.4 5.6 collective-permute-start.14
  368.8 5.7 collective-permute-start.8
  370.8 38.0 %collective-permute-start.18 = (bf16[32,1024]{1,0:T(8,128)(2,1)S(1)}, bf16[32,1024]{1,0:T(8,128)(2,1)}, u32[]{:S(2)}, u32[]{:S(2)}) collective-permute-start(bf16[32,1024]{1,0:T(8,128)(2,1)S(1)} %get-tuple-element.95), channel_id=1, source_target_pairs={{4,0},{8,4},{12,8},{16,12},{20,16},{24,20},{28,24},{0,28},{5,1},{9... | collective-permute-start | bytes 196616 | tf_op jit(solution)/shard_map/ppermute | solution.py:29
  371.5 37.4 %collective-permute-start.11 = (bf16[32,1024]{1,0:T(8,128)(2,1)S(1)}, bf16[32,1024]{1,0:T(8,128)(2,1)}, u32[]{:S(2)}, u32[]{:S(2)}) collective-permute-start(bf16[32,1024]{1,0:T(8,128)(2,1)S(1)} %get-tuple-element.92), channel_id=1, source_target_pairs={{4,0},{8,4},{12,8},{16,12},{20,16},{24,20},{28,24},{0,28},{5,1},{9... | collective-permute-start | bytes 196616 | tf_op jit(solution)/shard_map/ppermute | solution.py:29
  373.0 40.3 %collective-permute-start.15 = (bf16[32,1024]{1,0:T(8,128)(2,1)S(1)}, bf16[32,1024]{1,0:T(8,128)(2,1)}, u32[]{:S(2)}, u32[]{:S(2)}) collective-permute-start(bf16[32,1024]{1,0:T(8,128)(2,1)S(1)} %collective-permute-done.14), channel_id=1, source_target_pairs={{0,4},{4,8},{8,12},{12,16},{16,20},{20,24},{24,28},{28,0},{1,5},{5... | collective-permute-start | bytes 196616 | tf_op jit(solution)/shard_map/ppermute | solution.py:27
  374.5 38.8 %collective-permute-start.9 = (bf16[32,1024]{1,0:T(8,128)(2,1)S(1)}, bf16[32,1024]{1,0:T(8,128)(2,1)}, u32[]{:S(2)}, u32[]{:S(2)}) collective-permute-start(bf16[32,1024]{1,0:T(8,128)(2,1)S(1)} %collective-permute-done.8), channel_id=1, source_target_pairs={{0,4},{4,8},{8,12},{12,16},{16,20},{20,24},{24,28},{28,0},{1,5},{5... | collective-permute-start | bytes 196616 | tf_op jit(solution)/shard_map/ppermute | solution.py:27
  408.8 47.9 %collective-permute-start.19 = (bf16[32,1024]{1,0:T(8,128)(2,1)}, bf16[32,1024]{1,0:T(8,128)(2,1)}, u32[]{:S(2)}, u32[]{:S(2)}) collective-permute-start(bf16[32,1024]{1,0:T(8,128)(2,1)} %collective-permute-done.18), channel_id=1, source_target_pairs={{4,0},{8,4},{12,8},{16,12},{20,16},{24,20},{28,24},{0,28},{5,1},{9... | collective-permute-start | bytes 196616 | tf_op jit(solution)/shard_map/ppermute | solution.py:29
  409.0 47.7 %collective-permute-start.12 = (bf16[32,1024]{1,0:T(8,128)(2,1)}, bf16[32,1024]{1,0:T(8,128)(2,1)}, u32[]{:S(2)}, u32[]{:S(2)}) collective-permute-start(bf16[32,1024]{1,0:T(8,128)(2,1)} %collective-permute-done.11), channel_id=1, source_target_pairs={{4,0},{8,4},{12,8},{16,12},{20,16},{24,20},{28,24},{0,28},{5,1},{9... | collective-permute-start | bytes 196616 | tf_op jit(solution)/shard_map/ppermute | solution.py:29
  413.3 47.7 %collective-permute-start.16 = (bf16[32,1024]{1,0:T(8,128)(2,1)}, bf16[32,1024]{1,0:T(8,128)(2,1)}, u32[]{:S(2)}, u32[]{:S(2)}) collective-permute-start(bf16[32,1024]{1,0:T(8,128)(2,1)} %collective-permute-done.15), channel_id=1, source_target_pairs={{0,4},{4,8},{8,12},{12,16},{16,20},{20,24},{24,28},{28,0},{1,5},{5... | collective-permute-start | bytes 196616 | tf_op jit(solution)/shard_map/ppermute | solution.py:27
  413.3 47.7 %collective-permute-start.10 = (bf16[32,1024]{1,0:T(8,128)(2,1)}, bf16[32,1024]{1,0:T(8,128)(2,1)}, u32[]{:S(2)}, u32[]{:S(2)}) collective-permute-start(bf16[32,1024]{1,0:T(8,128)(2,1)} %collective-permute-done.9), channel_id=1, source_target_pairs={{0,4},{4,8},{8,12},{12,16},{16,20},{20,24},{24,28},{28,0},{1,5},{5... | collective-permute-start | bytes 196616 | tf_op jit(solution)/shard_map/ppermute | solution.py:27
  456.6 27.2 %collective-permute-start.20 = (bf16[32,1024]{1,0:T(8,128)(2,1)}, bf16[32,1024]{1,0:T(8,128)(2,1)}, u32[]{:S(2)}, u32[]{:S(2)}) collective-permute-start(bf16[32,1024]{1,0:T(8,128)(2,1)} %collective-permute-done.19), channel_id=1, source_target_pairs={{4,0},{8,4},{12,8},{16,12},{20,16},{24,20},{28,24},{0,28},{5,1},{9... | collective-permute-start | bytes 196616 | tf_op jit(solution)/shard_map/ppermute | solution.py:29
  456.7 24.1 %collective-permute-start.13 = (bf16[32,1024]{1,0:T(8,128)(2,1)}, bf16[32,1024]{1,0:T(8,128)(2,1)S(1)}, u32[]{:S(2)}, u32[]{:S(2)}) collective-permute-start(bf16[32,1024]{1,0:T(8,128)(2,1)} %collective-permute-done.12), channel_id=1, source_target_pairs={{4,0},{8,4},{12,8},{16,12},{20,16},{24,20},{28,24},{0,28},{5,1},{9... | collective-permute-start | bytes 196616 | tf_op jit(solution)/shard_map/ppermute | solution.py:29
  461.0 7.3 collective-permute-start.17
  560.6 133.3 %reduce-scatter.21.cloned.1.call-start = ((), (), s32[]{:S(2)}) async-start(), calls=%async_computation.19 | async-start | bytes 1179648 | tf_op jit(solution)/shard_map/reduce_scatter | solution.py:162
  569.8 189.9 %reduce-scatter.15.cloned.1.call-start = ((), (), s32[]{:S(2)}) async-start(), calls=%async_computation.16 | async-start | bytes 1179648 | tf_op jit(solution)/shard_map/reduce_scatter | solution.py:159
  572.8 253.0 %reduce-scatter.19.cloned.1.call-start = ((), (), s32[]{:S(2)}) async-start(), calls=%async_computation.18 | async-start | bytes 1179648 | tf_op jit(solution)/shard_map/reduce_scatter | solution.py:159
  577.8 370.3 %reduce-scatter.25.cloned.1.call-start = ((), (), s32[]{:S(2)}) async-start(), calls=%async_computation.21 | async-start | bytes 4325376 | tf_op jit(solution)/shard_map/reduce_scatter | solution.py:186
  581.7 544.8 %reduce-scatter.23.cloned.1.call-start = ((), (), s32[]{:S(2)}) async-start(), calls=%async_computation.20 | async-start | bytes 12976128 | tf_op jit(solution)/shard_map/reduce_scatter | solution.py:185
  833.4 480.5 %reduce-scatter.29.cloned.1.call-start = ((), (), s32[]{:S(2)}) async-start(), calls=%async_computation.23 | async-start | bytes 17301504 | tf_op jit(solution)/shard_map/reduce_scatter | solution.py:189
  845.0 656.2 %reduce-scatter.27.cloned.1.call-start = ((), (), s32[]{:S(2)}) async-start(), calls=%async_computation.22 | async-start | bytes 17301504 | tf_op jit(solution)/shard_map/reduce_scatter | solution.py:188
  (151 other events, 4215.8 us)
Sparse Core Ops, SparseCore 0:
  9.6 46.5 all-gather.5
  57.8 22.5 all-gather.7
  82.0 58.2 all-gather.9
  141.7 58.2 all-gather.11
  219.0 64.3 reduce-scatter.12
  287.0 62.4 reduce-scatter.10
  560.7 66.9 reduce-scatter.16
  631.4 62.3 reduce-scatter.20
  697.3 62.4 reduce-scatter.14
  763.4 62.4 reduce-scatter.18
  828.7 107.7 reduce-scatter.24
  943.0 183.5 reduce-scatter.22
  1129.5 184.4 reduce-scatter.28
  1316.8 184.4 reduce-scatter.26
